TPU v7x, 32 devices: a whole 2x2x4 slice. The times are simulated.
32 devices in a mesh: row: 16 (over z, x, core), col: 2 (over y).
Axes of the slice: x: 2, y: 2, z: 4, core: 2. Of those that a mesh axis runs over, the one named last changes fastest.
Arguments:
- g_occupied: bfloat16 [64, 512, 512], P(('row', 'col')), may hold values from -6 to 6
- g_virtual: bfloat16 [64, 512, 512], P(('row', 'col')), may hold values from -6 to 6
- owner: int32 [64, 1], P(('row', 'col')), may hold values from 0 to 1; in each aligned block of 2 rows (0 to 1, 2 to 3, ...) at most 2 rows name the same one
- coulomb: bfloat16 [1024, 3072], P('col', 'row'), may hold values from -0.25 to 0.25
Outputs:
- screened: bfloat16 [16384, 3072], P(('row', 'col'))
Inputs may be any that keep to these rules, and one draw needn't show every extreme that they name: `owner`: among the 2 pairs of one device, no tile column is named more than twice, and some device names one twice.
All inputs are finite; a program needn't handle non-finite values.
Results may differ from a plain program's by a relative error of at most 0.015.
Values may be sent and summed in bfloat16 or wider, within the bound.
No kernel may reach another device: no remote copies, remote signals or barrier semaphores. Data moves between devices by JAX's collectives and lax.ppermute only.
A program may use at most 64 MiB of HBM per device.

v0:
```python
import jax
import jax.numpy as jnp
from jax import lax
from jax.sharding import PartitionSpec as P


def body(g_occupied, g_virtual, owner, coulomb):
    n_col = lax.axis_size("col")
    pol = g_occupied.astype(jnp.float32) * g_virtual.astype(jnp.float32)
    targets = owner[:, 0]
    columns = jnp.arange(n_col, dtype=jnp.int32)
    onehot = (targets[:, None] == columns[None, :]).astype(jnp.float32)
    contrib = jnp.einsum("sd,sij->dij", onehot, pol).astype(jnp.bfloat16)
    received = lax.all_to_all(contrib, "col", split_axis=0, concat_axis=0, tiled=True)
    tile = jnp.sum(received.astype(jnp.float32), axis=0).astype(jnp.bfloat16)
    result = jnp.dot(
        tile, lax.all_gather(coulomb, "row", axis=1, tiled=True), preferred_element_type=jnp.float32
    )
    return result.astype(jnp.bfloat16)


def solution(mesh):
    return jax.shard_map(
        body,
        mesh=mesh,
        in_specs=(
            P(("row", "col"), None, None),
            P(("row", "col"), None, None),
            P(("row", "col"), None),
            P("col", "row"),
        ),
        out_specs=P(("row", "col"), None),
        check_vma=False,
    )
```

profile of v0, /device:TPU:0, one launch (start us, length us, event | category | flops | bytes accessed | tf_op | source)
XLA Modules:
  0.0 70.0 jit_solution(15090743242697294910)
XLA Ops:
  6.5 0.0 copy-start
  6.5 0.0 all-gather.2.cloned.1.call-start
  6.5 0.7 %all-gather.2.cloned.1.call-update = ((bf16[512,192]{0,1:T(8,128)(2,1)}), bf16[512,3072]{0,1:T(8,128)(2,1)}) async-update(((), (), s32[]{:S(2)}) %all-gather.2.cloned.1.call-start, bf16[512,192]{0,1:T(8,128)(2,1)} %param.7) | async-update | bytes 3538968
  7.3 1.8 %convert_multiply_fusion = bf16[2,512,512]{2,1,0:T(8,128)(2,1)S(1)} fusion(bf16[2,512,512]{2,1,0:T(8,128)(2,1)} %param.5, bf16[2,512,512]{2,1,0:T(8,128)(2,1)} %param.4), kind=kLoop, calls=%fused_computation.2 | loop fusion | flops 2097152 | bytes 3145728 | tf_op jit(solution)/shard_map/mul | solution.py:9
  9.1 0.0 copy-done
  9.1 1.9 %fusion = bf16[2,512,512]{2,0,1:T(2,128)(2,1)S(1)} fusion(bf16[2,512,512]{2,1,0:T(8,128)(2,1)S(1)} %convert_multiply_fusion, s32[2]{0:T(128)S(1)} %bitcast.6), kind=kOutput, calls=%fused_computation.3 | convolution fusion | flops 2097156 | bytes 2097160 | tf_op jit(solution)/shard_map/sd,sij->dij/dot_general | solution.py:13
  11.0 0.2 copy.10
  11.2 17.6 %all_to_all.5 = bf16[2,512,512]{2,1,0:T(8,128)(2,1)S(1)} all-to-all(bf16[2,512,512]{2,1,0:T(8,128)(2,1)S(1)} %copy.10), channel_id=1, replica_groups=mesh['row'=16,'col'=2] {'col'}, dimensions={0} | all-to-all | bytes 2097152 | tf_op jit(solution)/shard_map/all_to_all | solution.py:14
  28.8 0.5 reduce_sum.12
  29.3 28.5 %all-gather.2.cloned.1.call-done = bf16[512,3072]{0,1:T(8,128)(2,1)} async-done(((bf16[512,192]{0,1:T(8,128)(2,1)}), bf16[512,3072]{0,1:T(8,128)(2,1)}) %all-gather.2.cloned.1.call-update) | async-done | bytes 3145744 | tf_op jit(solution)/shard_map/all_gather | solution.py:17
  57.8 5.4 %convolution_convert_fusion = bf16[512,3072]{1,0:T(8,128)(2,1)} fusion(bf16[512,512]{1,0:T(8,128)(2,1)S(1)} %reduce_sum.12, bf16[512,3072]{0,1:T(8,128)(2,1)} %all-gather.2.cloned.1.call-done), kind=kOutput, calls=%fused_computation | convolution fusion | flops 1612185600 | bytes 6815744 | tf_op jit(solution)/shard_map/dot_general | solution.py:16
Async XLA Ops:
  6.5 2.6 %copy-start = (s32[2,1]{0,1:T(1,128)S(1)}, s32[2,1]{0,1:T(1,128)}, u32[]{:S(2)}) copy-start(s32[2,1]{0,1:T(1,128)} %param.6) | copy-start | bytes 28
  6.5 51.2 %all-gather.2.cloned.1.call-start = ((), (), s32[]{:S(2)}) async-start(), calls=%async_computation.1 | async-start | bytes 3342336 | tf_op jit(solution)/shard_map/all_gather | solution.py:17
Sparse Core Ops, SparseCore 0:
  9.6 48.0 all-gather.1
where the time goes:
time: 70.2 us; the launch traced here: 70 us
  waiting for transfers between devices  29.2 us (42%)
  blocking collectives  17.6 us (25%)
  between operations  13.4 us (19%)
  matrix products  7.25 us (10%)
  other arithmetic  2.32 us (3%)
    all_gather x1, waiting for transfers between devices, body(): lax.all_gather(coulomb, 'row', axis=1, tiled=True)  28.5 us
    all_to_all x1, blocking collectives, body(): lax.all_to_all(contrib, 'col', split_axis=0, concat_axis=0, tiled=True)  17.6 us
    dot_general x1, matrix products, body(): jnp.dot(tile, lax.all_gather(coulomb, 'row', axis=1, tiled=True), preferr...  5.38 us
    dot_general x1, matrix products, body(): contrib = jnp.einsum('sd,sij->dij', onehot, pol).astype(jnp.bfloat16)  1.87 us
    mul x1, other arithmetic, body(): pol = g_occupied.astype(jnp.float32) * g_virtual.astype(jnp.float32)  1.83 us
  transfers between devices with their start and end apart: 1, of which 1 were waited for; matrix products, arithmetic and copies ran while one was open for 6% of the time, Pallas kernels for 0%

commit v1 on v0

--- a/solution.py
+++ b/solution.py
@@ -2,6 +2,19 @@
 import jax.numpy as jnp
 from jax import lax
 from jax.sharding import PartitionSpec as P
+
+
+def gather_around(shard, axis, dim):
+    ways = lax.axis_size(axis)
+    up = [(d, (d + 1) % ways) for d in range(ways)]
+    down = [(d, (d - 1) % ways) for d in range(ways)]
+    earlier, later = ([shard], [shard])
+    for _ in range(ways // 2):
+        earlier.append(lax.ppermute(earlier[-1], axis, up))
+    for _ in range((ways - 1) // 2):
+        later.append(lax.ppermute(later[-1], axis, down))
+    line = jnp.concatenate([*earlier[::-1], *later[1:]], axis=dim)
+    return jnp.roll(line, (lax.axis_index(axis) - ways // 2) * shard.shape[dim], axis=dim)
 
 
 def body(g_occupied, g_virtual, owner, coulomb):
@@ -13,9 +26,7 @@
     contrib = jnp.einsum("sd,sij->dij", onehot, pol).astype(jnp.bfloat16)
     received = lax.all_to_all(contrib, "col", split_axis=0, concat_axis=0, tiled=True)
     tile = jnp.sum(received.astype(jnp.float32), axis=0).astype(jnp.bfloat16)
-    result = jnp.dot(
-        tile, lax.all_gather(coulomb, "row", axis=1, tiled=True), preferred_element_type=jnp.float32
-    )
+    result = jnp.dot(tile, gather_around(coulomb, "row", 1), preferred_element_type=jnp.float32)
     return result.astype(jnp.bfloat16)
 
 

time: 70.2 us -> 78.6 us (1.12)
  starting transfers between devices: 0.01 us -> 36.1 us
  blocking collectives: 17.6 us -> 0 us
  between operations: 13.4 us -> 0.3 us
  local copies, waits for them, and re-layouts: 0.17 us -> 7.19 us
  waiting for transfers between devices: 29.2 us -> 25.6 us
  matrix products: 7.25 us -> 6.08 us
    ppermute x0 -> x15, starting transfers between devices: none -> 32.5 us  [the longest x7 32.1 us: gather_around(): later.append(lax.ppermute(later[-1], axis, down))]
    all_gather x1 -> x0, waiting for transfers between devices: 28.5 us -> none  [body(): lax.all_gather(coulomb, 'row', axis=1, tiled=True)]
    ppermute x0 -> x15, waiting for transfers between devices: none -> 25.6 us  [the longest x8 20.3 us: gather_around(): earlier.append(lax.ppermute(earlier[-1], axis, up))]
    all_to_all x1 -> x0, blocking collectives: 17.6 us -> none  [body(): lax.all_to_all(contrib, 'col', split_axis=0, concat_axis=0, tiled=True)]
    unnamed x2 -> x35, local copies, waits for them, and re-layouts: 0.01 us -> 6.04 us
    all_to_all x0 -> x1, starting transfers between devices: none -> 3.58 us  [body(): lax.all_to_all(contrib, 'col', split_axis=0, concat_axis=0, tiled=True)]
    dot_general x1, matrix products: 5.38 us -> 3.53 us  [body(): jnp.dot(tile, gather_around(coulomb, 'row', 1), preferred_element_type=jn...]
    dot_general x1, local copies, waits for them, and re-layouts: 0.17 us -> 1.14 us  [body(): contrib = jnp.einsum('sd,sij->dij', onehot, pol).astype(jnp.bfloat16)]
  transfers between devices with their start and end apart: 1 -> 16, of which waited for: 1 -> 10; matrix products, arithmetic and copies ran while one was open for 6% -> 12% of each run, Pallas kernels for 0% -> 0%
where the time goes in v1:
time: 78.6 us; the launch traced here: 78.2 us
  starting transfers between devices  36.1 us (46%)
  waiting for transfers between devices  25.6 us (33%)
  local copies, waits for them, and re-layouts  7.19 us (9%)
  matrix products  6.08 us (8%)
  other arithmetic  2.94 us (4%)
    ppermute x7, starting transfers between devices, gather_around(): later.append(lax.ppermute(later[-1], axis, down))  32.1 us
    ppermute x8, waiting for transfers between devices, gather_around(): earlier.append(lax.ppermute(earlier[-1], axis, up))  20.3 us
    unnamed x35, local copies, waits for them, and re-layouts  6.04 us
    ppermute x7, waiting for transfers between devices, gather_around(): later.append(lax.ppermute(later[-1], axis, down))  5.25 us
    all_to_all x1, starting transfers between devices, body(): lax.all_to_all(contrib, 'col', split_axis=0, concat_axis=0, tiled=True)  3.58 us
    dot_general x1, matrix products, body(): jnp.dot(tile, gather_around(coulomb, 'row', 1), preferred_element_type=jn...  3.53 us
    dot_general x1, matrix products, body(): contrib = jnp.einsum('sd,sij->dij', onehot, pol).astype(jnp.bfloat16)  2.55 us
    mul x1, other arithmetic, body(): pol = g_occupied.astype(jnp.float32) * g_virtual.astype(jnp.float32)  1.83 us
  transfers between devices with their start and end apart: 16, of which 10 were waited for; matrix products, arithmetic and copies ran while one was open for 12% of the time, Pallas kernels for 0%

profile of v1, /device:TPU:0, one launch (start us, length us, event | category | flops | bytes accessed | tf_op | source)
XLA Modules:
  0.0 78.2 jit_solution(14028791862517968533)
XLA Ops:
  0.0 0.5 collective-permute-start
  0.5 8.5 %collective-permute-done = bf16[512,192]{0,1:T(8,128)(2,1)S(1)} collective-permute-done((bf16[512,192]{0,1:T(8,128)(2,1)}, bf16[512,192]{0,1:T(8,128)(2,1)S(1)}, u32[]{:S(2)}, u32[]{:S(2)}) %collective-permute-start) | collective-permute-done | bytes 196640 | tf_op jit(solution)/shard_map/ppermute | solution.py:13
  9.0 0.0 collective-permute-start.1
  9.0 4.4 %collective-permute-start.8 = (bf16[512,192]{0,1:T(8,128)(2,1)}, bf16[512,192]{0,1:T(8,128)(2,1)S(1)}, u32[]{:S(2)}, u32[]{:S(2)}) collective-permute-start(bf16[512,192]{0,1:T(8,128)(2,1)} %param.7), channel_id=1, source_target_pairs={{0,30},{2,0},{4,2},{6,4},{8,6},{10,8},{12,10},{14,12},{16,14},{18,... | collective-permute-start | bytes 589832 | tf_op jit(solution)/shard_map/ppermute | solution.py:15
  13.4 3.3 %collective-permute-done.1 = bf16[512,192]{0,1:T(8,128)(2,1)S(1)} collective-permute-done((bf16[512,192]{0,1:T(8,128)(2,1)S(1)}, bf16[512,192]{0,1:T(8,128)(2,1)S(1)}, u32[]{:S(2)}, u32[]{:S(2)}) %collective-permute-start.1) | collective-permute-done | bytes 196640 | tf_op jit(solution)/shard_map/ppermute | solution.py:13
  16.8 0.0 collective-permute-start.2
  16.8 0.2 collective-permute-done.8
  16.9 4.6 %collective-permute-start.9 = (bf16[512,192]{0,1:T(8,128)(2,1)S(1)}, bf16[512,192]{0,1:T(8,128)(2,1)S(1)}, u32[]{:S(2)}, u32[]{:S(2)}) collective-permute-start(bf16[512,192]{0,1:T(8,128)(2,1)S(1)} %collective-permute-done.8), channel_id=1, source_target_pairs={{0,30},{2,0},{4,2},{6,4},{8,6},{10,8},{12,10},{14,12},{16,14},{18,... | collective-permute-start | bytes 589832 | tf_op jit(solution)/shard_map/ppermute | solution.py:15
  21.5 3.1 %collective-permute-done.2 = bf16[512,192]{0,1:T(8,128)(2,1)S(1)} collective-permute-done((bf16[512,192]{0,1:T(8,128)(2,1)S(1)}, bf16[512,192]{0,1:T(8,128)(2,1)S(1)}, u32[]{:S(2)}, u32[]{:S(2)}) %collective-permute-start.2) | collective-permute-done | bytes 196640 | tf_op jit(solution)/shard_map/ppermute | solution.py:13
  24.7 0.0 collective-permute-start.3
  24.7 0.0 collective-permute-done.9
  24.7 4.7 %collective-permute-start.10 = (bf16[512,192]{0,1:T(8,128)(2,1)S(1)}, bf16[512,192]{0,1:T(8,128)(2,1)S(1)}, u32[]{:S(2)}, u32[]{:S(2)}) collective-permute-start(bf16[512,192]{0,1:T(8,128)(2,1)S(1)} %collective-permute-done.9), channel_id=1, source_target_pairs={{0,30},{2,0},{4,2},{6,4},{8,6},{10,8},{12,10},{14,12},{16,14},{18,... | collective-permute-start | bytes 589832 | tf_op jit(solution)/shard_map/ppermute | solution.py:15
  29.4 3.1 %collective-permute-done.3 = bf16[512,192]{0,1:T(8,128)(2,1)S(1)} collective-permute-done((bf16[512,192]{0,1:T(8,128)(2,1)S(1)}, bf16[512,192]{0,1:T(8,128)(2,1)S(1)}, u32[]{:S(2)}, u32[]{:S(2)}) %collective-permute-start.3) | collective-permute-done | bytes 196640 | tf_op jit(solution)/shard_map/ppermute | solution.py:13
  32.6 0.0 collective-permute-start.4
  32.6 1.8 %convert_multiply_fusion = bf16[2,512,512]{2,1,0:T(8,128)(2,1)S(1)} fusion(bf16[2,512,512]{2,1,0:T(8,128)(2,1)} %param.5, bf16[2,512,512]{2,1,0:T(8,128)(2,1)} %param.4), kind=kLoop, calls=%fused_computation.3 | loop fusion | flops 2097152 | bytes 3145728 | tf_op jit(solution)/shard_map/mul | solution.py:22
  34.4 0.0 collective-permute-done.10
  34.4 4.5 %collective-permute-start.11 = (bf16[512,192]{0,1:T(8,128)(2,1)S(1)}, bf16[512,192]{0,1:T(8,128)(2,1)S(1)}, u32[]{:S(2)}, u32[]{:S(2)}) collective-permute-start(bf16[512,192]{0,1:T(8,128)(2,1)S(1)} %collective-permute-done.10), channel_id=1, source_target_pairs={{0,30},{2,0},{4,2},{6,4},{8,6},{10,8},{12,10},{14,12},{16,14},{18,... | collective-permute-start | bytes 589832 | tf_op jit(solution)/shard_map/ppermute | solution.py:15
  38.9 1.4 %collective-permute-done.4 = bf16[512,192]{0,1:T(8,128)(2,1)S(1)} collective-permute-done((bf16[512,192]{0,1:T(8,128)(2,1)S(1)}, bf16[512,192]{0,1:T(8,128)(2,1)S(1)}, u32[]{:S(2)}, u32[]{:S(2)}) %collective-permute-start.4) | collective-permute-done | bytes 196640 | tf_op jit(solution)/shard_map/ppermute | solution.py:13
  40.4 0.0 collective-permute-start.5
  40.4 0.0 copy-start
  40.4 2.6 %fusion.1 = bf16[2,512,512]{2,0,1:T(2,128)(2,1)S(1)} fusion(bf16[2,512,512]{2,1,0:T(8,128)(2,1)S(1)} %convert_multiply_fusion, s32[2]{0:T(128)} %bitcast.5), kind=kOutput, calls=%fused_computation.4 | convolution fusion | flops 2097156 | bytes 2097160 | tf_op jit(solution)/shard_map/sd,sij->dij/dot_general | solution.py:26
  42.9 1.1 %copy.10 = bf16[2,512,512]{2,1,0:T(8,128)(2,1)} copy(bf16[2,512,512]{2,0,1:T(2,128)(2,1)S(1)} %fusion.1) | data formatting | bytes 2097152 | tf_op jit(solution)/shard_map/sd,sij->dij/dot_general | solution.py:26
  44.1 3.6 %all-to-all-start = ((bf16[2,512,512]{2,1,0:T(8,128)(2,1)}), bf16[2,512,512]{2,1,0:T(8,128)(2,1)S(1)}, u32[]{:S(2)}, u32[]{:S(2)}) async-start(bf16[2,512,512]{2,1,0:T(8,128)(2,1)} %copy.10), calls=%async_computation | async-start | bytes 2097152 | tf_op jit(solution)/shard_map/all_to_all | solution.py:27
  47.7 0.0 collective-permute-done.11
  47.7 4.5 %collective-permute-start.12 = (bf16[512,192]{0,1:T(8,128)(2,1)S(1)}, bf16[512,192]{0,1:T(8,128)(2,1)S(1)}, u32[]{:S(2)}, u32[]{:S(2)}) collective-permute-start(bf16[512,192]{0,1:T(8,128)(2,1)S(1)} %collective-permute-done.11), channel_id=1, source_target_pairs={{0,30},{2,0},{4,2},{6,4},{8,6},{10,8},{12,10},{14,12},{16,14},{18,... | collective-permute-start | bytes 589832 | tf_op jit(solution)/shard_map/ppermute | solution.py:15
  52.2 0.0 collective-permute-done.5
  52.2 0.0 collective-permute-start.6
  52.2 3.2 %collective-permute-done.12 = bf16[512,192]{0,1:T(8,128)(2,1)S(1)} collective-permute-done((bf16[512,192]{0,1:T(8,128)(2,1)S(1)}, bf16[512,192]{0,1:T(8,128)(2,1)S(1)}, u32[]{:S(2)}, u32[]{:S(2)}) %collective-permute-start.12) | collective-permute-done | bytes 196640 | tf_op jit(solution)/shard_map/ppermute | solution.py:15
  55.3 4.7 %collective-permute-start.13 = (bf16[512,192]{0,1:T(8,128)(2,1)S(1)}, bf16[512,192]{0,1:T(8,128)(2,1)S(1)}, u32[]{:S(2)}, u32[]{:S(2)}) collective-permute-start(bf16[512,192]{0,1:T(8,128)(2,1)S(1)} %collective-permute-done.12), channel_id=1, source_target_pairs={{0,30},{2,0},{4,2},{6,4},{8,6},{10,8},{12,10},{14,12},{16,14},{18,... | collective-permute-start | bytes 589832 | tf_op jit(solution)/shard_map/ppermute | solution.py:15
  60.1 0.2 collective-permute-done.6
  60.3 0.0 collective-permute-start.7
  60.3 0.0 all-to-all-done
  60.3 1.1 %reduce_sum.12 = bf16[512,512]{1,0:T(8,128)(2,1)} reduce(bf16[2,512,512]{2,1,0:T(8,128)(2,1)S(1)} %all-to-all-done, bf16[]{:T(256)} %constant.25.clone.1), dimensions={0}, to_apply=%region_0.0 | reduce | flops 262144 | bytes 1572866 | tf_op jit(solution)/shard_map/reduce_sum | solution.py:28
  61.4 0.0 copy-start.1
  61.4 1.9 %collective-permute-done.13 = bf16[512,192]{0,1:T(8,128)(2,1)S(1)} collective-permute-done((bf16[512,192]{0,1:T(8,128)(2,1)S(1)}, bf16[512,192]{0,1:T(8,128)(2,1)S(1)}, u32[]{:S(2)}, u32[]{:S(2)}) %collective-permute-start.13) | collective-permute-done | bytes 196640 | tf_op jit(solution)/shard_map/ppermute | solution.py:15
  63.2 4.6 %collective-permute-start.14 = (bf16[512,192]{0,1:T(8,128)(2,1)S(1)}, bf16[512,192]{0,1:T(8,128)(2,1)S(1)}, u32[]{:S(2)}, u32[]{:S(2)}) collective-permute-start(bf16[512,192]{0,1:T(8,128)(2,1)S(1)} %collective-permute-done.13), channel_id=1, source_target_pairs={{0,30},{2,0},{4,2},{6,4},{8,6},{10,8},{12,10},{14,12},{16,14},{18,... | collective-permute-start | bytes 589832 | tf_op jit(solution)/shard_map/ppermute | solution.py:15
  67.8 0.5 collective-permute-done.7
  68.4 0.9 %constant_dynamic-update-slice_fusion.31 = bf16[512,6144]{0,1:T(8,128)(2,1)S(1)} fusion(bf16[512,192]{0,1:T(8,128)(2,1)} %collective-permute-done.7), kind=kLoop, calls=%fused_computation.37 | loop fusion | bytes 393216
  69.3 0.9 %constant_dynamic-update-slice_fusion.30 = bf16[512,6144]{0,1:T(8,128)(2,1)S(1)} fusion(bf16[512,6144]{0,1:T(8,128)(2,1)S(1)} %constant_dynamic-update-slice_fusion.31, bf16[512,192]{0,1:T(8,128)(2,1)} %collective-permute-done.6), kind=kLoop, calls=%fused_computation.36 | loop fusion | bytes 393216
  70.3 0.9 %constant_dynamic-update-slice_fusion.29 = bf16[512,6144]{0,1:T(8,128)(2,1)S(1)} fusion(bf16[512,6144]{0,1:T(8,128)(2,1)S(1)} %constant_dynamic-update-slice_fusion.30, bf16[512,192]{0,1:T(8,128)(2,1)} %collective-permute-done.5), kind=kLoop, calls=%fused_computation.35 | loop fusion | bytes 393216
  71.3 0.0 copy-done
  71.5 0.0 collective-permute-done.14
  71.5 0.9 %constant_dynamic-update-slice_fusion.15 = bf16[512,6144]{0,1:T(8,128)(2,1)S(1)} fusion(bf16[512,6144]{0,1:T(8,128)(2,1)S(1)} %constant_dynamic-update-slice_fusion.16, bf16[512,192]{0,1:T(8,128)(2,1)} %collective-permute-done.7), kind=kLoop, calls=%fused_computation.21 | loop fusion | bytes 393216
  72.5 0.9 %constant_dynamic-update-slice_fusion.14 = bf16[512,6144]{0,1:T(8,128)(2,1)S(1)} fusion(bf16[512,6144]{0,1:T(8,128)(2,1)S(1)} %constant_dynamic-update-slice_fusion.15, bf16[512,192]{0,1:T(8,128)(2,1)} %collective-permute-done.6), kind=kLoop, calls=%fused_computation.20 | loop fusion | bytes 393216
  73.4 0.9 %constant_dynamic-update-slice_fusion.13 = bf16[512,6144]{0,1:T(8,128)(2,1)S(1)} fusion(bf16[512,6144]{0,1:T(8,128)(2,1)S(1)} %constant_dynamic-update-slice_fusion.14, bf16[512,192]{0,1:T(8,128)(2,1)} %collective-permute-done.5), kind=kLoop, calls=%fused_computation.19 | loop fusion | bytes 393216
  74.7 0.0 copy-done.1
  74.7 3.5 %convolution_convert_fusion = bf16[512,3072]{1,0:T(8,128)(2,1)} fusion(bf16[512,512]{1,0:T(8,128)(2,1)S(1)} %copy-done.1, bf16[512,6144]{0,1:T(8,128)(2,1)S(1)} %constant_dynamic-update-slice_fusion, s32[]{:T(128)S(6)} %select_n.14), kind=kOutput, calls=%fused_computation | convolution fusion | flops 1612185600 | bytes 6815748 | tf_op jit(solution)/shard_map/dot_general | solution.py:29
  (26 shorter events, 0.4 us)
Async XLA Ops:
  0.0 9.0 %collective-permute-start = (bf16[512,192]{0,1:T(8,128)(2,1)}, bf16[512,192]{0,1:T(8,128)(2,1)S(1)}, u32[]{:S(2)}, u32[]{:S(2)}) collective-permute-start(bf16[512,192]{0,1:T(8,128)(2,1)} %param.7), channel_id=1, source_target_pairs={{0,2},{2,4},{4,6},{6,8},{8,10},{10,12},{12,14},{14,16},{16,18},{18... | collective-permute-start | bytes 589832 | tf_op jit(solution)/shard_map/ppermute | solution.py:13
  9.0 7.8 %collective-permute-start.1 = (bf16[512,192]{0,1:T(8,128)(2,1)S(1)}, bf16[512,192]{0,1:T(8,128)(2,1)S(1)}, u32[]{:S(2)}, u32[]{:S(2)}) collective-permute-start(bf16[512,192]{0,1:T(8,128)(2,1)S(1)} %collective-permute-done), channel_id=1, source_target_pairs={{0,2},{2,4},{4,6},{6,8},{8,10},{10,12},{12,14},{14,16},{16,18},{18... | collective-permute-start | bytes 589832 | tf_op jit(solution)/shard_map/ppermute | solution.py:13
  9.0 7.9 %collective-permute-start.8 = (bf16[512,192]{0,1:T(8,128)(2,1)}, bf16[512,192]{0,1:T(8,128)(2,1)S(1)}, u32[]{:S(2)}, u32[]{:S(2)}) collective-permute-start(bf16[512,192]{0,1:T(8,128)(2,1)} %param.7), channel_id=1, source_target_pairs={{0,30},{2,0},{4,2},{6,4},{8,6},{10,8},{12,10},{14,12},{16,14},{18,... | collective-permute-start | bytes 589832 | tf_op jit(solution)/shard_map/ppermute | solution.py:15
  16.8 7.9 %collective-permute-start.2 = (bf16[512,192]{0,1:T(8,128)(2,1)S(1)}, bf16[512,192]{0,1:T(8,128)(2,1)S(1)}, u32[]{:S(2)}, u32[]{:S(2)}) collective-permute-start(bf16[512,192]{0,1:T(8,128)(2,1)S(1)} %collective-permute-done.1), channel_id=1, source_target_pairs={{0,2},{2,4},{4,6},{6,8},{8,10},{10,12},{12,14},{14,16},{16,18},{18... | collective-permute-start | bytes 589832 | tf_op jit(solution)/shard_map/ppermute | solution.py:13
  16.9 7.8 %collective-permute-start.9 = (bf16[512,192]{0,1:T(8,128)(2,1)S(1)}, bf16[512,192]{0,1:T(8,128)(2,1)S(1)}, u32[]{:S(2)}, u32[]{:S(2)}) collective-permute-start(bf16[512,192]{0,1:T(8,128)(2,1)S(1)} %collective-permute-done.8), channel_id=1, source_target_pairs={{0,30},{2,0},{4,2},{6,4},{8,6},{10,8},{12,10},{14,12},{16,14},{18,... | collective-permute-start | bytes 589832 | tf_op jit(solution)/shard_map/ppermute | solution.py:15
  24.7 7.9 %collective-permute-start.3 = (bf16[512,192]{0,1:T(8,128)(2,1)S(1)}, bf16[512,192]{0,1:T(8,128)(2,1)S(1)}, u32[]{:S(2)}, u32[]{:S(2)}) collective-permute-start(bf16[512,192]{0,1:T(8,128)(2,1)S(1)} %collective-permute-done.2), channel_id=1, source_target_pairs={{0,2},{2,4},{4,6},{6,8},{8,10},{10,12},{12,14},{14,16},{16,18},{18... | collective-permute-start | bytes 589832 | tf_op jit(solution)/shard_map/ppermute | solution.py:13
  24.7 9.7 %collective-permute-start.10 = (bf16[512,192]{0,1:T(8,128)(2,1)S(1)}, bf16[512,192]{0,1:T(8,128)(2,1)S(1)}, u32[]{:S(2)}, u32[]{:S(2)}) collective-permute-start(bf16[512,192]{0,1:T(8,128)(2,1)S(1)} %collective-permute-done.9), channel_id=1, source_target_pairs={{0,30},{2,0},{4,2},{6,4},{8,6},{10,8},{12,10},{14,12},{16,14},{18,... | collective-permute-start | bytes 589832 | tf_op jit(solution)/shard_map/ppermute | solution.py:15
  32.6 7.8 %collective-permute-start.4 = (bf16[512,192]{0,1:T(8,128)(2,1)S(1)}, bf16[512,192]{0,1:T(8,128)(2,1)S(1)}, u32[]{:S(2)}, u32[]{:S(2)}) collective-permute-start(bf16[512,192]{0,1:T(8,128)(2,1)S(1)} %collective-permute-done.3), channel_id=1, source_target_pairs={{0,2},{2,4},{4,6},{6,8},{8,10},{10,12},{12,14},{14,16},{16,18},{18... | collective-permute-start | bytes 589832 | tf_op jit(solution)/shard_map/ppermute | solution.py:13
  34.4 13.2 %collective-permute-start.11 = (bf16[512,192]{0,1:T(8,128)(2,1)S(1)}, bf16[512,192]{0,1:T(8,128)(2,1)S(1)}, u32[]{:S(2)}, u32[]{:S(2)}) collective-permute-start(bf16[512,192]{0,1:T(8,128)(2,1)S(1)} %collective-permute-done.10), channel_id=1, source_target_pairs={{0,30},{2,0},{4,2},{6,4},{8,6},{10,8},{12,10},{14,12},{16,14},{18,... | collective-permute-start | bytes 589832 | tf_op jit(solution)/shard_map/ppermute | solution.py:15
  40.4 11.8 %collective-permute-start.5 = (bf16[512,192]{0,1:T(8,128)(2,1)S(1)}, bf16[512,192]{0,1:T(8,128)(2,1)}, u32[]{:S(2)}, u32[]{:S(2)}) collective-permute-start(bf16[512,192]{0,1:T(8,128)(2,1)S(1)} %collective-permute-done.4), channel_id=1, source_target_pairs={{0,2},{2,4},{4,6},{6,8},{8,10},{10,12},{12,14},{14,16},{16,18},{18... | collective-permute-start | bytes 589832 | tf_op jit(solution)/shard_map/ppermute | solution.py:13
  40.4 31.0 %copy-start = (bf16[512,192]{0,1:T(8,128)(2,1)S(1)}, bf16[512,192]{0,1:T(8,128)(2,1)}, u32[]{:S(2)}) copy-start(bf16[512,192]{0,1:T(8,128)(2,1)} %param.7) | copy-start | bytes 589828
  44.1 16.2 %all-to-all-start = ((bf16[2,512,512]{2,1,0:T(8,128)(2,1)}), bf16[2,512,512]{2,1,0:T(8,128)(2,1)S(1)}, u32[]{:S(2)}, u32[]{:S(2)}) async-start(bf16[2,512,512]{2,1,0:T(8,128)(2,1)} %copy.10), calls=%async_computation | async-start | bytes 2097152 | tf_op jit(solution)/shard_map/all_to_all | solution.py:27
  47.7 7.7 %collective-permute-start.12 = (bf16[512,192]{0,1:T(8,128)(2,1)S(1)}, bf16[512,192]{0,1:T(8,128)(2,1)S(1)}, u32[]{:S(2)}, u32[]{:S(2)}) collective-permute-start(bf16[512,192]{0,1:T(8,128)(2,1)S(1)} %collective-permute-done.11), channel_id=1, source_target_pairs={{0,30},{2,0},{4,2},{6,4},{8,6},{10,8},{12,10},{14,12},{16,14},{18,... | collective-permute-start | bytes 589832 | tf_op jit(solution)/shard_map/ppermute | solution.py:15
  52.2 8.1 %collective-permute-start.6 = (bf16[512,192]{0,1:T(8,128)(2,1)}, bf16[512,192]{0,1:T(8,128)(2,1)}, u32[]{:S(2)}, u32[]{:S(2)}) collective-permute-start(bf16[512,192]{0,1:T(8,128)(2,1)} %collective-permute-done.5), channel_id=1, source_target_pairs={{0,2},{2,4},{4,6},{6,8},{8,10},{10,12},{12,14},{14,16},{16,18},{18... | collective-permute-start | bytes 589832 | tf_op jit(solution)/shard_map/ppermute | solution.py:13
  55.3 7.9 %collective-permute-start.13 = (bf16[512,192]{0,1:T(8,128)(2,1)S(1)}, bf16[512,192]{0,1:T(8,128)(2,1)S(1)}, u32[]{:S(2)}, u32[]{:S(2)}) collective-permute-start(bf16[512,192]{0,1:T(8,128)(2,1)S(1)} %collective-permute-done.12), channel_id=1, source_target_pairs={{0,30},{2,0},{4,2},{6,4},{8,6},{10,8},{12,10},{14,12},{16,14},{18,... | collective-permute-start | bytes 589832 | tf_op jit(solution)/shard_map/ppermute | solution.py:15
  60.3 8.1 %collective-permute-start.7 = (bf16[512,192]{0,1:T(8,128)(2,1)}, bf16[512,192]{0,1:T(8,128)(2,1)}, u32[]{:S(2)}, u32[]{:S(2)}) collective-permute-start(bf16[512,192]{0,1:T(8,128)(2,1)} %collective-permute-done.6), channel_id=1, source_target_pairs={{0,2},{2,4},{4,6},{6,8},{8,10},{10,12},{12,14},{14,16},{16,18},{18... | collective-permute-start | bytes 589832 | tf_op jit(solution)/shard_map/ppermute | solution.py:13
  61.4 13.3 %copy-start.1 = (bf16[512,512]{1,0:T(8,128)(2,1)S(1)}, bf16[512,512]{1,0:T(8,128)(2,1)}, u32[]{:S(2)}) copy-start(bf16[512,512]{1,0:T(8,128)(2,1)} %reduce_sum.12) | copy-start | bytes 1572868
  63.2 8.3 %collective-permute-start.14 = (bf16[512,192]{0,1:T(8,128)(2,1)S(1)}, bf16[512,192]{0,1:T(8,128)(2,1)S(1)}, u32[]{:S(2)}, u32[]{:S(2)}) collective-permute-start(bf16[512,192]{0,1:T(8,128)(2,1)S(1)} %collective-permute-done.13), channel_id=1, source_target_pairs={{0,30},{2,0},{4,2},{6,4},{8,6},{10,8},{12,10},{14,12},{16,14},{18,... | collective-permute-start | bytes 589832 | tf_op jit(solution)/shard_map/ppermute | solution.py:15
